TPU v7x, 32 devices: a whole 2x2x4 slice. The times are simulated.
32 devices in a mesh: dp: 8 (over z, x), ctx: 4 (over y, core).
Axes of the slice: x: 2, y: 2, z: 4, core: 2. Of those that a mesh axis runs over, the one named last changes fastest.
Arguments:
- inputs: bfloat16 [8, 512, 5376], P('dp', 'ctx'), may hold values from -6 to 6
- q_proj: bfloat16 [8, 512, 2048], P('dp', 'ctx'), may hold values from -260 to 260
- k_proj: bfloat16 [8, 512, 1024], P('dp', 'ctx'), may hold values from -260 to 260
- v_proj: bfloat16 [8, 512, 1024], P('dp', 'ctx'), may hold values from -6 to 6
- d_attn: bfloat16 [8, 512, 2048], P('dp', 'ctx'), may hold values from -6 to 6
- positions: int32 [8, 512], P('dp', 'ctx'), may hold values from 0 to 511, as said below
- windows: int32 [8], P('dp'), may hold values from 512 to 1024
- q_gain: float32 [128], replicated, may hold values from 0.7 to 5.5
- k_gain: float32 [128], replicated, may hold values from 0.7 to 5.5
- weight: bfloat16 [5376, 4096], P('dp'), may hold values from -0.078125 to 0.078125
Outputs:
- d_inputs: bfloat16 [8, 512, 5376], P('dp', 'ctx')
- d_weight_t: float32 [4096, 5376], P('ctx', 'dp')
- d_q_gain: float32 [128], replicated
- d_k_gain: float32 [128], replicated
Inputs may be any that keep to these rules, and one draw needn't show every extreme that they name: `positions`: within each sequence a position counts the tokens since its document began: it grows by one from token to token and falls to 0 where a document begins; the first token of a sequence has position 0. Some sequence holds a single document.
All inputs are finite; a program needn't handle non-finite values.
Results may differ from a plain program's by a relative error of at most 0.029.
Values may be sent and summed in bfloat16 or wider, within the bound.
A program may use at most 128 MiB of HBM per device.

v0:
```python
import math
import jax
import jax.numpy as jnp
from jax import lax
from jax.sharding import PartitionSpec as P

REACH = 8
score_scale = 168.0 ** (-0.5)
rope_base = 10000.0
norm_eps = 1e-06


def from_behind(value, axis, steps):
    count = lax.axis_size(axis)
    initial, last = (max(0, -steps), min(count, count - steps))
    return lax.ppermute(value, axis, [(source, source + steps) for source in range(initial, last)])


def rotated_unit(projected_rows, gain_vector, token_pos, head_count):
    head_width = gain_vector.shape[0]
    rows_heads = projected_rows.reshape(projected_rows.shape[0], head_count, head_width)
    inverse = lax.rsqrt(jnp.mean(rows_heads * rows_heads, axis=-1, keepdims=True) + norm_eps)
    normed = rows_heads * inverse * gain_vector
    half_width = head_width // 2
    frequency = jnp.exp(
        jnp.arange(half_width, dtype=jnp.float32) * (-2.0 * math.log(rope_base) / head_width)
    )
    angles = token_pos.astype(jnp.float32)[:, None] * frequency[None, :]
    cosine_table = jnp.cos(angles)[:, None, :]
    sine_table = jnp.sin(angles)[:, None, :]
    first_half = normed[..., :half_width]
    second_half = normed[..., half_width:]
    return jnp.concatenate(
        [
            first_half * cosine_table - second_half * sine_table,
            second_half * cosine_table + first_half * sine_table,
        ],
        axis=-1,
    )


def shards(inputs, q_proj, k_proj, v_proj, d_attn, positions, windows, q_gain, k_gain, weight):
    tok_rows = inputs.shape[1]
    head_width = q_gain.shape[0]
    query_heads = q_proj.shape[2] // head_width
    key_heads = k_proj.shape[2] // head_width
    group_size = query_heads // key_heads
    token_pos = positions[0]
    window = windows[0]
    input_cols = lax.all_to_all(inputs, "dp", split_axis=2, concat_axis=0, tiled=True)

    def query_side(projected_rows, gain_vector):
        return rotated_unit(projected_rows, gain_vector, token_pos, query_heads)

    def key_side(projected_rows, gain_vector):
        return rotated_unit(projected_rows, gain_vector, token_pos, key_heads)

    q_full, query_back = jax.vjp(query_side, q_proj[0].astype(jnp.float32), q_gain)
    k_full, key_back = jax.vjp(key_side, k_proj[0].astype(jnp.float32), k_gain)
    query_rotated = q_full.astype(jnp.bfloat16).reshape(tok_rows, key_heads, group_size, head_width)
    key_rotated = k_full.astype(jnp.bfloat16)
    v_own = v_proj[0].reshape(tok_rows, key_heads, head_width)
    reach_count = min(REACH, lax.axis_size("ctx") - 1)
    key_blocks = [key_rotated]
    value_blocks = [v_own]
    for distance_steps in range(1, reach_count + 1):
        far_keys, far_values = from_behind((key_rotated, v_own), "ctx", distance_steps)
        key_blocks.append(far_keys)
        value_blocks.append(far_values)
    all_keys = jnp.stack(key_blocks)
    all_values = jnp.stack(value_blocks)
    block_ids = jnp.arange(reach_count + 1, dtype=jnp.int32)
    offsets = jnp.arange(tok_rows, dtype=jnp.int32)
    distance = block_ids[None, :, None] * tok_rows + offsets[:, None, None] - offsets[None, None, :]
    allowed = (distance >= 0) & (distance < window) & (distance <= token_pos[:, None, None])
    scores = (
        jnp.einsum("ahgd,bchd->hgabc", query_rotated, all_keys, preferred_element_type=jnp.float32)
        * score_scale
    )
    scores = jnp.where(allowed, scores, -jnp.inf)
    row_max = jnp.max(scores, axis=(3, 4), keepdims=True)
    exponent = jnp.exp(scores - row_max)
    probs = exponent / jnp.sum(exponent, axis=(3, 4), keepdims=True)
    head_gradient = d_attn[0].reshape(tok_rows, key_heads, group_size, head_width)
    dprobs = jnp.einsum(
        "ahgd,bchd->hgabc", head_gradient, all_values, preferred_element_type=jnp.float32
    )
    delta = jnp.sum(probs * dprobs, axis=(3, 4), keepdims=True)
    dscores = (probs * (dprobs - delta)).astype(jnp.bfloat16)
    probs_low = probs.astype(jnp.bfloat16)
    dq_rot = (
        jnp.einsum("hgabc,bchd->ahgd", dscores, all_keys, preferred_element_type=jnp.float32)
        * score_scale
    )
    dk_blocks = (
        jnp.einsum("hgabc,ahgd->bchd", dscores, query_rotated, preferred_element_type=jnp.float32)
        * score_scale
    )
    dv_blocks = jnp.einsum(
        "hgabc,ahgd->bchd", probs_low, head_gradient, preferred_element_type=jnp.float32
    )
    dk_total = dk_blocks[0]
    dv_total = dv_blocks[0]
    for distance_steps in range(1, reach_count + 1):
        back_keys, back_values = from_behind(
            (
                dk_blocks[distance_steps].astype(jnp.bfloat16),
                dv_blocks[distance_steps].astype(jnp.bfloat16),
            ),
            "ctx",
            -distance_steps,
        )
        dk_total = dk_total + back_keys.astype(jnp.float32)
        dv_total = dv_total + back_values.astype(jnp.float32)
    dq_proj, dq_gain = query_back(dq_rot.reshape(tok_rows, query_heads, head_width))
    dk_proj, dk_gain = key_back(dk_total)
    dq_gain_all, dk_gain_all = lax.psum((dq_gain, dk_gain), ("dp", "ctx"))
    dv_proj = dv_total.reshape(tok_rows, key_heads * head_width)
    d_proj = jnp.concatenate([dq_proj, dk_proj, dv_proj], axis=-1).astype(jnp.bfloat16)[None]
    gathered = lax.all_gather(d_proj, "dp", axis=0, tiled=True)
    d_cols = jnp.einsum("btp,dp->btd", gathered, weight, preferred_element_type=jnp.float32)
    d_inputs = lax.all_to_all(
        d_cols.astype(jnp.bfloat16), "dp", split_axis=0, concat_axis=2, tiled=True
    )
    d_weight_t = lax.psum_scatter(
        jnp.einsum("btp,btd->pd", gathered, input_cols, preferred_element_type=jnp.float32).astype(
            jnp.bfloat16
        ),
        "ctx",
        scatter_dimension=0,
        tiled=True,
    ).astype(jnp.float32)
    return (d_inputs, d_weight_t, dq_gain_all, dk_gain_all)


def solution(mesh):
    placed = (
        P("dp", "ctx", None),
        P("dp", "ctx", None),
        P("dp", "ctx", None),
        P("dp", "ctx", None),
        P("dp", "ctx", None),
        P("dp", "ctx"),
        P("dp"),
        P(),
        P(),
        P("dp", None),
    )
    return jax.shard_map(
        shards,
        mesh=mesh,
        in_specs=placed,
        out_specs=(P("dp", "ctx", None), P("ctx", "dp"), P(), P()),
        check_vma=False,
    )
```

profile of v0, /device:TPU:0, one launch (start us, length us, event | category | flops | bytes accessed | tf_op | source)
XLA Modules:
  0.0 321.0 jit_solution(8718791477971543858)
XLA Ops:
  11.7 5.0 %collective-permute-start.2 = (bf16[128,8,128]{2,0,1:T(8,128)(2,1)}, bf16[128,8,128]{2,0,1:T(8,128)(2,1)}, u32[]{:S(2)}, u32[]{:S(2)}) collective-permute-start(bf16[128,8,128]{2,0,1:T(8,128)(2,1)} %pad_maximum_fusion.3), channel_id=1, source_target_pairs={{0,3},{4,7},{8,11},{12,15},{16,19},{20,23},{24,27},{28,31}} | collective-permute-start | bytes 786440 | tf_op jit(solution)/shard_map/ppermute | solution.py:16
  16.7 2.0 collective-permute-start
  18.7 2.0 collective-permute-start.1
  21.7 2.0 collective-permute-start.3
  23.6 2.0 collective-permute-start.4
  28.5 1.4 reshape_squeeze.7
  31.4 1.5 collective-permute-start.5
  32.9 2.1 fusion.7
  35.9 3.9 %collective-permute-done.5 = bf16[128,8,128]{2,0,1:T(8,128)(2,1)S(1)} collective-permute-done((bf16[128,8,128]{2,0,1:T(8,128)(2,1)}, bf16[128,8,128]{2,0,1:T(8,128)(2,1)S(1)}, u32[]{:S(2)}, u32[]{:S(2)}) %collective-permute-start.5) | collective-permute-done | bytes 262176 | tf_op jit(solution)/shard_map/ppermute | solution.py:16
  39.8 2.4 fusion.2
  43.6 1.7 fusion.21
  45.2 2.2 fusion.57
  47.4 3.0 fusion.56
  50.5 1.4 copy.237
  51.9 1.4 copy.238
  58.1 1.8 multiply_add_fusion.1
  60.9 1.8 fusion.22
  69.3 1.7 collective-permute-done.8
  74.0 2.3 collective-permute-done.10
  76.3 6.4 %collective-permute-done.11 = bf16[128,8,128]{0,2,1:T(8,128)(2,1)S(1)} collective-permute-done((bf16[128,8,128]{0,2,1:T(8,128)(2,1)S(1)}, bf16[128,8,128]{0,2,1:T(8,128)(2,1)S(1)}, u32[]{:S(2)}, u32[]{:S(2)}) %collective-permute-start.11) | collective-permute-done | bytes 262176 | tf_op jit(solution)/shard_map/ppermute | solution.py:16
  85.4 6.3 %copy.211 = bf16[1,128,5376]{1,0,2:T(2,128)(2,1)S(1)} copy(bf16[1,128,5376]{2,1,0:T(8,128)(2,1)} %param.10) | data formatting | bytes 2752512 | tf_op args[0]
  92.2 30.3 %reduce = bf16[5376,128]{1,0:T(8,128)(2,1)} reduce(bf16[5376,1,128]{2,1,0:T(2,128)(2,1)S(1)} %bitcast.178, bf16[]{:T(256)} %broadcast.142), dimensions={1}, to_apply=%bitcast.157.reduce_sub_computation | reduce | bytes 2752514
  122.4 3.2 %reshape.256 = bf16[8,2,43008]{2,1,0:T(2,128)(2,1)S(1)} reshape(bf16[5376,128]{1,0:T(8,128)(2,1)} %reduce) | data formatting | bytes 2752512
  125.7 71.0 %all_to_all.36 = bf16[8,2,43008]{2,1,0:T(2,128)(2,1)} all-to-all(bf16[8,2,43008]{2,1,0:T(2,128)(2,1)S(1)} %reshape.256), channel_id=1, replica_groups=mesh['dp'=8,'ctx'=4] {'dp'}, dimensions={0} | all-to-all | bytes 2752512 | tf_op jit(solution)/shard_map/all_to_all | solution.py:50
  196.7 4.5 %reshape.257 = bf16[5376,1,128]{2,1,0:T(2,128)(2,1)S(1)} reshape(bf16[8,2,43008]{2,1,0:T(2,128)(2,1)} %all_to_all.36) | data formatting | bytes 2752512
  202.5 29.1 %all-gather.2.cloned.1.call-done = bf16[8,128,4096]{2,1,0:T(8,128)(2,1)} async-done(((bf16[1,128,4096]{2,1,0:T(8,128)(2,1)}), bf16[8,128,4096]{2,1,0:T(8,128)(2,1)}) %all-gather.2.cloned.1.call-update) | async-done | bytes 8388624 | tf_op jit(solution)/shard_map/all_gather | solution.py:120
  231.6 10.2 %bitcast_convert_fusion = bf16[4096,672]{0,1:T(8,128)(2,1)} fusion(bf16[8,128,672]{1,2,0:T(8,128)(2,1)} %bitcast.192, bf16[8,128,4096]{2,1,0:T(8,128)(2,1)} %all-gather.2.cloned.1.call-done), kind=kOutput, calls=%fused_computation | convolution fusion | flops 5639897088 | bytes 15269888 | tf_op jit(solution)/shard_map/btp,btd->pd/dot_general | solution.py:126
  241.8 11.1 %fusion.18 = bf16[8,128,672]{1,2,0:T(8,128)(2,1)} fusion(bf16[8,128,4096]{2,1,0:T(8,128)(2,1)} %all-gather.2.cloned.1.call-done, bf16[672,4096]{1,0:T(8,128)(2,1)} %param.19), kind=kOutput, calls=%fused_computation.20 | convolution fusion | flops 5637832704 | bytes 15269888 | tf_op jit(solution)/shard_map/btp,dp->btd/dot_general | solution.py:121
  252.9 3.6 %all-to-all-start = ((bf16[8,128,672]{1,2,0:T(8,128)(2,1)}), bf16[8,128,672]{1,2,0:T(8,128)(2,1)S(1)}, u32[]{:S(2)}, u32[]{:S(2)}) async-start(bf16[8,128,672]{1,2,0:T(8,128)(2,1)} %fusion.18), calls=%async_computation | async-start | bytes 2752512 | tf_op jit(solution)/shard_map/all_to_all | solution.py:122
  256.4 53.0 %all-reduce.4 = (f32[128]{0:T(128)}, f32[128]{0:T(128)}) all-reduce(f32[128]{0:T(128)S(1)} %get-tuple-element.28, f32[128]{0:T(128)S(1)} %get-tuple-element.30), channel_id=1, replica_groups=mesh['dp'=8,'ctx'=4] {'dp','ctx'}, use_global_device_ids=true, to_apply=%region_9.10 | all-reduce | flops 256 | bytes 2048 | tf_op jit(solution)/shard_map/psum | solution.py:117
  309.5 1.5 copy.212
  311.0 3.2 %convert_element_type.126 = f32[1024,672]{0,1:T(8,128)} convert(bf16[1024,672]{0,1:T(8,128)(2,1)} %reduce-scatter.2.cloned.1.call-done) | non-fusion elementwise | flops 688128 | bytes 4128768 | tf_op jit(solution)/shard_map/convert_element_type | solution.py:132
  (86 shorter events, 31.2 us)
Async XLA Ops:
  7.2 13.5 %copy-start.4 = (bf16[1,128,1024]{2,1,0:T(8,128)(2,1)S(1)}, bf16[1,128,1024]{2,1,0:T(8,128)(2,1)}, u32[]{:S(2)}) copy-start(bf16[1,128,1024]{2,1,0:T(8,128)(2,1)} %param.13) | copy-start | bytes 786436
  7.2 18.5 %copy-start.2 = (bf16[1,128,2048]{2,1,0:T(8,128)(2,1)S(1)}, bf16[1,128,2048]{2,1,0:T(8,128)(2,1)}, u32[]{:S(2)}) copy-start(bf16[1,128,2048]{2,1,0:T(8,128)(2,1)} %param.11) | copy-start | bytes 1572868
  7.2 224.4 %all-gather.2.cloned.1.call-start = ((), (), s32[]{:S(2)}) async-start(), calls=%async_computation.3 | async-start | bytes 9437184 | tf_op jit(solution)/shard_map/all_gather | solution.py:120
  8.6 17.0 %copy-start = (f32[128,8,128]{2,0,1:T(8,128)}, f32[128,8,128]{2,0,1:T(8,128)S(1)}, u32[]{:S(2)}) copy-start(f32[128,8,128]{2,0,1:T(8,128)S(1)} %copy.177) | copy-start | bytes 1572868
  10.5 15.9 %copy-start.5 = (f32[128]{0:T(128)S(1)}, f32[128]{0:T(128)}, u32[]{:S(2)}) copy-start(f32[128]{0:T(128)} %param.17) | copy-start | bytes 1540
  11.7 19.7 %collective-permute-start.2 = (bf16[128,8,128]{2,0,1:T(8,128)(2,1)}, bf16[128,8,128]{2,0,1:T(8,128)(2,1)}, u32[]{:S(2)}, u32[]{:S(2)}) collective-permute-start(bf16[128,8,128]{2,0,1:T(8,128)(2,1)} %pad_maximum_fusion.3), channel_id=1, source_target_pairs={{0,3},{4,7},{8,11},{12,15},{16,19},{20,23},{24,27},{28,31}} | collective-permute-start | bytes 786440 | tf_op jit(solution)/shard_map/ppermute | solution.py:16
  16.7 16.2 %collective-permute-start = (bf16[128,8,128]{2,0,1:T(8,128)(2,1)}, bf16[128,8,128]{2,0,1:T(8,128)(2,1)}, u32[]{:S(2)}, u32[]{:S(2)}) collective-permute-start(bf16[128,8,128]{2,0,1:T(8,128)(2,1)} %pad_maximum_fusion.3), channel_id=1, source_target_pairs={{0,1},{1,2},{2,3},{4,5},{5,6},{6,7},{8,9},{9,10},{10,11},{12,13},{... | collective-permute-start | bytes 786440 | tf_op jit(solution)/shard_map/ppermute | solution.py:16
  18.7 14.3 %collective-permute-start.1 = (bf16[128,8,128]{2,0,1:T(8,128)(2,1)}, bf16[128,8,128]{2,0,1:T(8,128)(2,1)}, u32[]{:S(2)}, u32[]{:S(2)}) collective-permute-start(bf16[128,8,128]{2,0,1:T(8,128)(2,1)} %pad_maximum_fusion.3), channel_id=1, source_target_pairs={{0,2},{1,3},{4,6},{5,7},{8,10},{9,11},{12,14},{13,15},{16,18},{17,... | collective-permute-start | bytes 786440 | tf_op jit(solution)/shard_map/ppermute | solution.py:16
  21.7 14.2 %collective-permute-start.3 = (bf16[128,8,128]{2,0,1:T(8,128)(2,1)}, bf16[128,8,128]{2,0,1:T(8,128)(2,1)}, u32[]{:S(2)}, u32[]{:S(2)}) collective-permute-start(bf16[128,8,128]{2,0,1:T(8,128)(2,1)} %copy.187), channel_id=1, source_target_pairs={{0,1},{1,2},{2,3},{4,5},{5,6},{6,7},{8,9},{9,10},{10,11},{12,13},{... | collective-permute-start | bytes 786440 | tf_op jit(solution)/shard_map/ppermute | solution.py:16
  23.6 12.3 %collective-permute-start.4 = (bf16[128,8,128]{2,0,1:T(8,128)(2,1)}, bf16[128,8,128]{2,0,1:T(8,128)(2,1)}, u32[]{:S(2)}, u32[]{:S(2)}) collective-permute-start(bf16[128,8,128]{2,0,1:T(8,128)(2,1)} %copy.187), channel_id=1, source_target_pairs={{0,2},{1,3},{4,6},{5,7},{8,10},{9,11},{12,14},{13,15},{16,18},{17,... | collective-permute-start | bytes 786440 | tf_op jit(solution)/shard_map/ppermute | solution.py:16
  26.8 4.5 %copy-start.7 = (s32[1,128]{1,0:T(1,128)S(1)}, s32[1,128]{1,0:T(1,128)}, u32[]{:S(2)}) copy-start(s32[1,128]{1,0:T(1,128)} %param.15) | copy-start | bytes 1540
  31.4 8.4 %collective-permute-start.5 = (bf16[128,8,128]{2,0,1:T(8,128)(2,1)}, bf16[128,8,128]{2,0,1:T(8,128)(2,1)S(1)}, u32[]{:S(2)}, u32[]{:S(2)}) collective-permute-start(bf16[128,8,128]{2,0,1:T(8,128)(2,1)} %copy.187), channel_id=1, source_target_pairs={{0,3},{4,7},{8,11},{12,15},{16,19},{20,23},{24,27},{28,31}} | collective-permute-start | bytes 786440 | tf_op jit(solution)/shard_map/ppermute | solution.py:16
  35.0 4.8 %copy-start.3 = (bf16[128,8,2,128,1]{0,3,2,4,1:T(8,128)(2,1)S(1)}, bf16[128,8,2,128,1]{0,3,2,4,1:T(8,128)(2,1)}, u32[]{:S(2)}) copy-start(bf16[128,8,2,128,1]{0,3,2,4,1:T(8,128)(2,1)} %copy.224) | copy-start | bytes 1572868
  54.2 13.7 %collective-permute-start.6 = (bf16[128,8,128]{2,0,1:T(8,128)(2,1)}, bf16[128,8,128]{2,0,1:T(8,128)(2,1)}, u32[]{:S(2)}, u32[]{:S(2)}) collective-permute-start(bf16[128,8,128]{2,0,1:T(8,128)(2,1)} %get-tuple-element.40), channel_id=1, source_target_pairs={{1,0},{2,1},{3,2},{5,4},{6,5},{7,6},{9,8},{10,9},{11,10},{13,12},{... | collective-permute-start | bytes 786440 | tf_op jit(solution)/shard_map/ppermute | solution.py:16
  55.5 13.8 %collective-permute-start.7 = (bf16[128,8,128]{2,0,1:T(8,128)(2,1)}, bf16[128,8,128]{2,0,1:T(8,128)(2,1)}, u32[]{:S(2)}, u32[]{:S(2)}) collective-permute-start(bf16[128,8,128]{2,0,1:T(8,128)(2,1)} %get-tuple-element.42), channel_id=1, source_target_pairs={{2,0},{3,1},{6,4},{7,5},{10,8},{11,9},{14,12},{15,13},{18,16},{19,... | collective-permute-start | bytes 786440 | tf_op jit(solution)/shard_map/ppermute | solution.py:16
  56.8 14.2 %collective-permute-start.8 = (bf16[128,8,128]{2,0,1:T(8,128)(2,1)}, bf16[128,8,128]{2,0,1:T(8,128)(2,1)}, u32[]{:S(2)}, u32[]{:S(2)}) collective-permute-start(bf16[128,8,128]{2,0,1:T(8,128)(2,1)} %get-tuple-element.41), channel_id=1, source_target_pairs={{3,0},{7,4},{11,8},{15,12},{19,16},{23,20},{27,24},{31,28}} | collective-permute-start | bytes 786440 | tf_op jit(solution)/shard_map/ppermute | solution.py:16
  62.7 9.9 %copy-start.1 = (f32[128,8,128]{2,0,1:T(8,128)S(1)}, f32[128,8,128]{2,0,1:T(8,128)}, u32[]{:S(2)}) copy-start(f32[128,8,128]{2,0,1:T(8,128)} %copy-done) | copy-start | bytes 1572868
  62.7 9.9 %copy-start.6 = (f32[128]{0:T(128)S(1)}, f32[128]{0:T(128)}, u32[]{:S(2)}) copy-start(f32[128]{0:T(128)} %param.18) | copy-start | bytes 1540
  65.2 11.1 %collective-permute-start.10 = (bf16[128,8,128]{0,2,1:T(8,128)(2,1)S(1)}, bf16[128,8,128]{0,2,1:T(8,128)(2,1)S(1)}, u32[]{:S(2)}, u32[]{:S(2)}) collective-permute-start(bf16[128,8,128]{0,2,1:T(8,128)(2,1)S(1)} %get-tuple-element.45), channel_id=1, source_target_pairs={{2,0},{3,1},{6,4},{7,5},{10,8},{11,9},{14,12},{15,13},{18,16},{19,... | collective-permute-start | bytes 786440 | tf_op jit(solution)/shard_map/ppermute | solution.py:16
  66.5 16.2 %collective-permute-start.11 = (bf16[128,8,128]{0,2,1:T(8,128)(2,1)S(1)}, bf16[128,8,128]{0,2,1:T(8,128)(2,1)S(1)}, u32[]{:S(2)}, u32[]{:S(2)}) collective-permute-start(bf16[128,8,128]{0,2,1:T(8,128)(2,1)S(1)} %get-tuple-element.44), channel_id=1, source_target_pairs={{3,0},{7,4},{11,8},{15,12},{19,16},{23,20},{27,24},{31,28}} | collective-permute-start | bytes 786440 | tf_op jit(solution)/shard_map/ppermute | solution.py:16
  67.8 14.9 %collective-permute-start.9 = (bf16[128,8,128]{0,2,1:T(8,128)(2,1)S(1)}, bf16[128,8,128]{0,2,1:T(8,128)(2,1)S(1)}, u32[]{:S(2)}, u32[]{:S(2)}) collective-permute-start(bf16[128,8,128]{0,2,1:T(8,128)(2,1)S(1)} %get-tuple-element.43), channel_id=1, source_target_pairs={{1,0},{2,1},{3,2},{5,4},{6,5},{7,6},{9,8},{10,9},{11,10},{13,12},{... | collective-permute-start | bytes 786440 | tf_op jit(solution)/shard_map/ppermute | solution.py:16
  85.1 225.9 %reduce-scatter.2.cloned.1.call-start = ((), (), s32[]{:S(2)}) async-start(), calls=%async_computation.4 | async-start | bytes 6881280 | tf_op jit(solution)/shard_map/reduce_scatter | solution.py:125
  252.9 56.6 %all-to-all-start = ((bf16[8,128,672]{1,2,0:T(8,128)(2,1)}), bf16[8,128,672]{1,2,0:T(8,128)(2,1)S(1)}, u32[]{:S(2)}, u32[]{:S(2)}) async-start(bf16[8,128,672]{1,2,0:T(8,128)(2,1)} %fusion.18), calls=%async_computation | async-start | bytes 2752512 | tf_op jit(solution)/shard_map/all_to_all | solution.py:122
Sparse Core Ops, SparseCore 0:
  85.2 146.3 all-gather.1
  241.9 51.8 reduce-scatter.1
where the time goes:
time: 322 us; the launch traced here: 321 us
  blocking collectives  124 us (39%)
  other arithmetic  49.7 us (15%)
  waiting for transfers between devices  43.6 us (14%)
  matrix products  32.5 us (10%)
  local copies, waits for them, and re-layouts  30 us (9%)
  starting transfers between devices  26 us (8%)
  between operations  15.2 us (5%)
    all_to_all x1, blocking collectives, shards(): lax.all_to_all(inputs, 'dp', split_axis=2, concat_axis=0, tiled=True)  71 us
    psum x1, blocking collectives, shards(): dq_gain_all, dk_gain_all = lax.psum((dq_gain, dk_gain), ('dp', 'ctx'))  53 us
    unnamed x2, other arithmetic  30.4 us
    all_gather x1, waiting for transfers between devices, shards(): gathered = lax.all_gather(d_proj, 'dp', axis=0, tiled=True)  29.1 us
    ppermute x12, starting transfers between devices, from_behind(): lax.ppermute(value, axis, [(source, source + steps) for source in range(i...  22.2 us
    unnamed x27, local copies, waits for them, and re-layouts  21.7 us
    ppermute x12, waiting for transfers between devices, from_behind(): lax.ppermute(value, axis, [(source, source + steps) for source in range(i...  14.4 us
    dot_general x1, matrix products, shards(): jnp.einsum('btp,dp->btd', gathered, weight, preferred_element_type=jnp.fl...  11.1 us
  transfers between devices with their start and end apart: 15, of which 6 were waited for; matrix products, arithmetic and copies ran while one was open for 24% of the time, Pallas kernels for 0%

commit v1 on v0

--- a/solution.py
+++ b/solution.py
@@ -8,6 +8,18 @@
 score_scale = 168.0 ** (-0.5)
 rope_base = 10000.0
 norm_eps = 1e-06
+
+
+def gather_by_bits(shard, axis, dim):
+    ways, here, lap = (lax.axis_size(axis), lax.axis_index(axis), shard.shape[dim])
+    line, have = (shard, 1)
+    while have < ways:
+        line = jnp.concatenate(
+            [line, lax.ppermute(line, axis, [(d, (d - have) % ways) for d in range(ways)])],
+            axis=dim,
+        )
+        have = 2 * have
+    return jnp.roll(line, here * lap, axis=dim)
 
 
 def from_behind(value, axis, steps):
@@ -117,7 +129,7 @@
     dq_gain_all, dk_gain_all = lax.psum((dq_gain, dk_gain), ("dp", "ctx"))
     dv_proj = dv_total.reshape(tok_rows, key_heads * head_width)
     d_proj = jnp.concatenate([dq_proj, dk_proj, dv_proj], axis=-1).astype(jnp.bfloat16)[None]
-    gathered = lax.all_gather(d_proj, "dp", axis=0, tiled=True)
+    gathered = gather_by_bits(d_proj, "dp", 0)
     d_cols = jnp.einsum("btp,dp->btd", gathered, weight, preferred_element_type=jnp.float32)
     d_inputs = lax.all_to_all(
         d_cols.astype(jnp.bfloat16), "dp", split_axis=0, concat_axis=2, tiled=True

time: 322 us -> 491 us (1.52)
  waiting for transfers between devices: 43.6 us -> 238 us
  blocking collectives: 124 us -> 55.1 us
  local copies, waits for them, and re-layouts: 30 us -> 50.2 us
  starting transfers between devices: 26 us -> 43.9 us
  other arithmetic: 49.7 us -> 55.2 us
    all_to_all x0 -> x1, waiting for transfers between devices: none -> 158 us  [shards(): lax.all_to_all(inputs, 'dp', split_axis=2, concat_axis=0, tiled=True)]
    all_to_all x1 -> x0, blocking collectives: 71 us -> none  [shards(): lax.all_to_all(inputs, 'dp', split_axis=2, concat_axis=0, tiled=True)]
    ppermute x0 -> x3, waiting for transfers between devices: none -> 66.5 us  [gather_by_bits(): lax.ppermute(line, axis, [(d, (d - have) % ways) for d in range(ways)])]
    all_gather x1 -> x0, waiting for transfers between devices: 29.1 us -> none  [shards(): gathered = lax.all_gather(d_proj, 'dp', axis=0, tiled=True)]
    unnamed x27 -> x44, local copies, waits for them, and re-layouts: 21.7 us -> 35.2 us
    all_to_all x0 -> x1, starting transfers between devices: none -> 8.28 us  [shards(): lax.all_to_all(inputs, 'dp', split_axis=2, concat_axis=0, tiled=True)]
    ppermute x0 -> x3, starting transfers between devices: none -> 6.66 us  [gather_by_bits(): lax.ppermute(line, axis, [(d, (d - have) % ways) for d in range(ways)])]
    unnamed x2 -> x3, other arithmetic: 30.4 us -> 32.5 us
  transfers between devices with their start and end apart: 15 -> 18, of which waited for: 6 -> 8; matrix products, arithmetic and copies ran while one was open for 24% -> 17% of each run, Pallas kernels for 0% -> 0%
where the time goes in v1:
time: 491 us; the launch traced here: 490 us
  waiting for transfers between devices  238 us (48%)
  other arithmetic  55.2 us (11%)
  blocking collectives  55.1 us (11%)
  local copies, waits for them, and re-layouts  50.2 us (10%)
  starting transfers between devices  43.9 us (9%)
  matrix products  32.5 us (7%)
  between operations  15.2 us (3%)
    all_to_all x1, waiting for transfers between devices, shards(): lax.all_to_all(inputs, 'dp', split_axis=2, concat_axis=0, tiled=True)  158 us
    ppermute x3, waiting for transfers between devices, gather_by_bits(): lax.ppermute(line, axis, [(d, (d - have) % ways) for d in range(ways)])  66.5 us
    psum x1, blocking collectives, shards(): dq_gain_all, dk_gain_all = lax.psum((dq_gain, dk_gain), ('dp', 'ctx'))  55.1 us
    unnamed x44, local copies, waits for them, and re-layouts  35.2 us
    unnamed x3, other arithmetic  32.5 us
    ppermute x12, starting transfers between devices, from_behind(): lax.ppermute(value, axis, [(source, source + steps) for source in range(i...  22.2 us
    ppermute x12, waiting for transfers between devices, from_behind(): lax.ppermute(value, axis, [(source, source + steps) for source in range(i...  13.6 us
    dot_general x1, matrix products, shards(): jnp.einsum('btp,dp->btd', gathered, weight, preferred_element_type=jnp.fl...  10.8 us
  transfers between devices with their start and end apart: 18, of which 8 were waited for; matrix products, arithmetic and copies ran while one was open for 17% of the time, Pallas kernels for 0%

profile of v1, /device:TPU:0, one launch (start us, length us, event | category | flops | bytes accessed | tf_op | source)
XLA Modules:
  0.0 489.8 jit_solution(1606946103892107766)
XLA Ops:
  10.9 5.0 %collective-permute-start.2 = (bf16[128,8,128]{2,0,1:T(8,128)(2,1)S(1)}, bf16[128,8,128]{2,0,1:T(8,128)(2,1)}, u32[]{:S(2)}, u32[]{:S(2)}) collective-permute-start(bf16[128,8,128]{2,0,1:T(8,128)(2,1)S(1)} %pad_maximum_fusion.5), channel_id=1, source_target_pairs={{0,3},{4,7},{8,11},{12,15},{16,19},{20,23},{24,27},{28,31}} | collective-permute-start | bytes 786440 | tf_op jit(solution)/shard_map/ppermute | solution.py:28
  15.9 2.0 collective-permute-start
  17.9 2.0 collective-permute-start.1
  21.0 2.0 collective-permute-start.3
  23.0 2.0 collective-permute-start.4
  33.6 2.1 fusion.12
  36.7 2.2 collective-permute-done.5
  38.9 2.4 fusion.7
  44.4 2.5 fusion.66
  46.8 3.0 fusion.65
  52.7 1.8 multiply_add_fusion.1
  55.6 2.0 slice_bitcast_fusion.7
  70.2 3.7 collective-permute-done.8
  78.0 6.3 %collective-permute-done.11 = bf16[128,8,128]{0,2,1:T(8,128)(2,1)S(1)} collective-permute-done((bf16[128,8,128]{0,2,1:T(8,128)(2,1)S(1)}, bf16[128,8,128]{0,2,1:T(8,128)(2,1)S(1)}, u32[]{:S(2)}, u32[]{:S(2)}) %collective-permute-start.11) | collective-permute-done | bytes 262176 | tf_op jit(solution)/shard_map/ppermute | solution.py:28
  86.7 4.5 collective-permute-start.12
  91.3 22.0 %collective-permute-done.12 = bf16[1,128,4096]{2,1,0:T(8,128)(2,1)S(1)} collective-permute-done((bf16[1,128,4096]{2,1,0:T(8,128)(2,1)S(1)}, bf16[1,128,4096]{2,1,0:T(8,128)(2,1)S(1)}, u32[]{:S(2)}, u32[]{:S(2)}) %collective-permute-start.12) | collective-permute-done | bytes 1048608 | tf_op jit(solution)/shard_map/ppermute | solution.py:18
  115.0 44.5 %collective-permute-done.13 = bf16[2,128,4096]{2,1,0:T(8,128)(2,1)S(1)} collective-permute-done((bf16[2,128,4096]{2,1,0:T(8,128)(2,1)S(1)}, bf16[2,128,4096]{2,1,0:T(8,128)(2,1)S(1)}, u32[]{:S(2)}, u32[]{:S(2)}) %collective-permute-start.13) | collective-permute-done | bytes 2097184 | tf_op jit(solution)/shard_map/ppermute | solution.py:18
  159.5 3.1 pad_maximum_fusion
  163.2 6.8 %copy.211 = bf16[1,128,5376]{1,0,2:T(2,128)(2,1)} copy(bf16[1,128,5376]{2,1,0:T(8,128)(2,1)} %param.10) | data formatting | bytes 2752512 | tf_op args[0]
  170.5 31.3 %reduce = bf16[5376,128]{1,0:T(8,128)(2,1)} reduce(bf16[5376,1,128]{2,1,0:T(2,128)(2,1)} %bitcast.176, bf16[]{:T(256)} %broadcast.143), dimensions={1}, to_apply=%bitcast.157.reduce_sub_computation | reduce | bytes 2752514
  201.8 4.1 reshape.256
  205.9 8.3 %all-to-all-start.1 = ((bf16[8,2,43008]{2,1,0:T(2,128)(2,1)}), bf16[8,2,43008]{2,1,0:T(2,128)(2,1)}, u32[]{:S(2)}, u32[]{:S(2)}) async-start(bf16[8,2,43008]{2,1,0:T(2,128)(2,1)} %reshape.256), calls=%async_computation.1 | async-start | bytes 2752512 | tf_op jit(solution)/shard_map/all_to_all | solution.py:62
  215.5 157.7 %all-to-all-done.1 = bf16[8,2,43008]{2,1,0:T(2,128)(2,1)} async-done(((bf16[8,2,43008]{2,1,0:T(2,128)(2,1)}), bf16[8,2,43008]{2,1,0:T(2,128)(2,1)}, u32[]{:S(2)}, u32[]{:S(2)}) %all-to-all-start.1) | async-done | bytes 1376288 | tf_op jit(solution)/shard_map/all_to_all | solution.py:62
  373.3 6.1 %reshape.257 = bf16[5376,1,128]{2,1,0:T(2,128)(2,1)} reshape(bf16[8,2,43008]{2,1,0:T(2,128)(2,1)} %all-to-all-done.1) | data formatting | bytes 2752512
  379.4 2.0 copy.236
  382.8 4.7 constant_dynamic-update-slice_fusion.4
  391.2 4.6 constant_dynamic-update-slice_fusion
  395.8 10.0 %bitcast_convert_fusion = bf16[4096,672]{0,1:T(8,128)(2,1)} fusion(bf16[8,128,672]{1,2,0:T(8,128)(2,1)S(1)} %bitcast.190, bf16[16,128,4096]{2,1,0:T(8,128)(2,1)} %constant_dynamic-update-slice_fusion, s32[]{:T(128)S(6)} %select_n.19), kind=kOutput, calls=%fused_computation | convolution fusion | flops 5639897088 | bytes 15269892 | tf_op jit(solution)/shard_map/btp,btd->pd/dot_general | solution.py:138
  405.9 10.8 %fusion.23 = bf16[8,128,672]{1,2,0:T(8,128)(2,1)} fusion(bf16[672,4096]{1,0:T(8,128)(2,1)} %param.19, bf16[16,128,4096]{2,1,0:T(8,128)(2,1)} %constant_dynamic-update-slice_fusion, s32[]{:T(128)S(6)} %select_n.19), kind=kOutput, calls=%fused_computation.25 | convolution fusion | flops 5637832704 | bytes 15269892 | tf_op jit(solution)/shard_map/btp,dp->btd/dot_general | solution.py:133
  416.7 6.5 %all-to-all-start = ((bf16[8,128,672]{1,2,0:T(8,128)(2,1)}), bf16[8,128,672]{1,2,0:T(8,128)(2,1)S(1)}, u32[]{:S(2)}, u32[]{:S(2)}) async-start(bf16[8,128,672]{1,2,0:T(8,128)(2,1)} %fusion.23), calls=%async_computation | async-start | bytes 2752512 | tf_op jit(solution)/shard_map/all_to_all | solution.py:134
  423.1 55.1 %all-reduce.4 = (f32[128]{0:T(128)}, f32[128]{0:T(128)}) all-reduce(f32[128]{0:T(128)S(1)} %get-tuple-element.28, f32[128]{0:T(128)S(1)} %get-tuple-element.30), channel_id=1, replica_groups=mesh['dp'=8,'ctx'=4] {'dp','ctx'}, use_global_device_ids=true, to_apply=%region_9.10 | all-reduce | flops 256 | bytes 2048 | tf_op jit(solution)/shard_map/psum | solution.py:129
  479.7 3.2 convert_element_type.126
  (111 shorter events, 50.2 us)
Async XLA Ops:
  7.2 12.8 %copy-start.9 = (bf16[1,128,1024]{2,1,0:T(8,128)(2,1)S(1)}, bf16[1,128,1024]{2,1,0:T(8,128)(2,1)}, u32[]{:S(2)}) copy-start(bf16[1,128,1024]{2,1,0:T(8,128)(2,1)} %param.13) | copy-start | bytes 786436
  7.2 17.8 %copy-start.6 = (bf16[1,128,2048]{2,1,0:T(8,128)(2,1)S(1)}, bf16[1,128,2048]{2,1,0:T(8,128)(2,1)}, u32[]{:S(2)}) copy-start(bf16[1,128,2048]{2,1,0:T(8,128)(2,1)} %param.11) | copy-start | bytes 1572868
  8.6 16.4 %copy-start.2 = (f32[128,8,128]{2,0,1:T(8,128)}, f32[128,8,128]{2,0,1:T(8,128)S(1)}, u32[]{:S(2)}) copy-start(f32[128,8,128]{2,0,1:T(8,128)S(1)} %copy.177) | copy-start | bytes 1572868
  10.5 15.3 %copy-start.11 = (f32[128]{0:T(128)S(1)}, f32[128]{0:T(128)}, u32[]{:S(2)}) copy-start(f32[128]{0:T(128)} %param.17) | copy-start | bytes 1540
  10.9 21.2 %collective-permute-start.2 = (bf16[128,8,128]{2,0,1:T(8,128)(2,1)S(1)}, bf16[128,8,128]{2,0,1:T(8,128)(2,1)}, u32[]{:S(2)}, u32[]{:S(2)}) collective-permute-start(bf16[128,8,128]{2,0,1:T(8,128)(2,1)S(1)} %pad_maximum_fusion.5), channel_id=1, source_target_pairs={{0,3},{4,7},{8,11},{12,15},{16,19},{20,23},{24,27},{28,31}} | collective-permute-start | bytes 786440 | tf_op jit(solution)/shard_map/ppermute | solution.py:28
  15.9 17.6 %collective-permute-start = (bf16[128,8,128]{2,0,1:T(8,128)(2,1)S(1)}, bf16[128,8,128]{2,0,1:T(8,128)(2,1)}, u32[]{:S(2)}, u32[]{:S(2)}) collective-permute-start(bf16[128,8,128]{2,0,1:T(8,128)(2,1)S(1)} %pad_maximum_fusion.5), channel_id=1, source_target_pairs={{0,1},{1,2},{2,3},{4,5},{5,6},{6,7},{8,9},{9,10},{10,11},{12,13},{... | collective-permute-start | bytes 786440 | tf_op jit(solution)/shard_map/ppermute | solution.py:28
  17.9 15.7 %collective-permute-start.1 = (bf16[128,8,128]{2,0,1:T(8,128)(2,1)S(1)}, bf16[128,8,128]{2,0,1:T(8,128)(2,1)}, u32[]{:S(2)}, u32[]{:S(2)}) collective-permute-start(bf16[128,8,128]{2,0,1:T(8,128)(2,1)S(1)} %pad_maximum_fusion.5), channel_id=1, source_target_pairs={{0,2},{1,3},{4,6},{5,7},{8,10},{9,11},{12,14},{13,15},{16,18},{17,... | collective-permute-start | bytes 786440 | tf_op jit(solution)/shard_map/ppermute | solution.py:28
  21.0 15.7 %collective-permute-start.3 = (bf16[128,8,128]{2,0,1:T(8,128)(2,1)}, bf16[128,8,128]{2,0,1:T(8,128)(2,1)}, u32[]{:S(2)}, u32[]{:S(2)}) collective-permute-start(bf16[128,8,128]{2,0,1:T(8,128)(2,1)} %copy.187), channel_id=1, source_target_pairs={{0,1},{1,2},{2,3},{4,5},{5,6},{6,7},{8,9},{9,10},{10,11},{12,13},{... | collective-permute-start | bytes 786440 | tf_op jit(solution)/shard_map/ppermute | solution.py:28
  23.0 13.7 %collective-permute-start.4 = (bf16[128,8,128]{2,0,1:T(8,128)(2,1)}, bf16[128,8,128]{2,0,1:T(8,128)(2,1)}, u32[]{:S(2)}, u32[]{:S(2)}) collective-permute-start(bf16[128,8,128]{2,0,1:T(8,128)(2,1)} %copy.187), channel_id=1, source_target_pairs={{0,2},{1,3},{4,6},{5,7},{8,10},{9,11},{12,14},{13,15},{16,18},{17,... | collective-permute-start | bytes 786440 | tf_op jit(solution)/shard_map/ppermute | solution.py:28
  26.1 5.9 %copy-start.13 = (s32[1,128]{1,0:T(1,128)S(1)}, s32[1,128]{1,0:T(1,128)}, u32[]{:S(2)}) copy-start(s32[1,128]{1,0:T(1,128)} %param.15) | copy-start | bytes 1540
  32.1 6.8 %collective-permute-start.5 = (bf16[128,8,128]{2,0,1:T(8,128)(2,1)}, bf16[128,8,128]{2,0,1:T(8,128)(2,1)S(1)}, u32[]{:S(2)}, u32[]{:S(2)}) collective-permute-start(bf16[128,8,128]{2,0,1:T(8,128)(2,1)} %copy.187), channel_id=1, source_target_pairs={{0,3},{4,7},{8,11},{12,15},{16,19},{20,23},{24,27},{28,31}} | collective-permute-start | bytes 786440 | tf_op jit(solution)/shard_map/ppermute | solution.py:28
  35.8 3.1 copy-start.7
  35.8 3.1 copy-start.10
  41.3 1.4 copy-start.8
  57.7 11.0 %collective-permute-start.6 = (bf16[128,8,128]{2,0,1:T(8,128)(2,1)}, bf16[128,8,128]{2,0,1:T(8,128)(2,1)}, u32[]{:S(2)}, u32[]{:S(2)}) collective-permute-start(bf16[128,8,128]{2,0,1:T(8,128)(2,1)} %get-tuple-element.42), channel_id=1, source_target_pairs={{1,0},{2,1},{3,2},{5,4},{6,5},{7,6},{9,8},{10,9},{11,10},{13,12},{... | collective-permute-start | bytes 786440 | tf_op jit(solution)/shard_map/ppermute | solution.py:28
  58.9 11.2 %collective-permute-start.7 = (bf16[128,8,128]{2,0,1:T(8,128)(2,1)}, bf16[128,8,128]{2,0,1:T(8,128)(2,1)}, u32[]{:S(2)}, u32[]{:S(2)}) collective-permute-start(bf16[128,8,128]{2,0,1:T(8,128)(2,1)} %get-tuple-element.44), channel_id=1, source_target_pairs={{2,0},{3,1},{6,4},{7,5},{10,8},{11,9},{14,12},{15,13},{18,16},{19,... | collective-permute-start | bytes 786440 | tf_op jit(solution)/shard_map/ppermute | solution.py:28
  60.2 13.6 %collective-permute-start.8 = (bf16[128,8,128]{2,0,1:T(8,128)(2,1)}, bf16[128,8,128]{2,0,1:T(8,128)(2,1)}, u32[]{:S(2)}, u32[]{:S(2)}) collective-permute-start(bf16[128,8,128]{2,0,1:T(8,128)(2,1)} %get-tuple-element.43), channel_id=1, source_target_pairs={{3,0},{7,4},{11,8},{15,12},{19,16},{23,20},{27,24},{31,28}} | collective-permute-start | bytes 786440 | tf_op jit(solution)/shard_map/ppermute | solution.py:28
  63.3 12.2 %copy-start.3 = (f32[128,8,128]{2,0,1:T(8,128)S(1)}, f32[128,8,128]{2,0,1:T(8,128)}, u32[]{:S(2)}) copy-start(f32[128,8,128]{2,0,1:T(8,128)} %copy-done.2) | copy-start | bytes 1572868
  63.3 12.2 %copy-start.12 = (f32[128]{0:T(128)S(1)}, f32[128]{0:T(128)}, u32[]{:S(2)}) copy-start(f32[128]{0:T(128)} %param.18) | copy-start | bytes 1540
  64.7 48.6 %copy-start = (bf16[1,128,2048]{2,1,0:T(8,128)(2,1)}, bf16[1,128,2048]{2,1,0:T(8,128)(2,1)S(1)}, u32[]{:S(2)}) copy-start(bf16[1,128,2048]{2,1,0:T(8,128)(2,1)S(1)} %concatenate.65) | copy-start | bytes 1572868
  66.0 11.9 %collective-permute-start.10 = (bf16[128,8,128]{0,2,1:T(8,128)(2,1)S(1)}, bf16[128,8,128]{0,2,1:T(8,128)(2,1)S(1)}, u32[]{:S(2)}, u32[]{:S(2)}) collective-permute-start(bf16[128,8,128]{0,2,1:T(8,128)(2,1)S(1)} %get-tuple-element.47), channel_id=1, source_target_pairs={{2,0},{3,1},{6,4},{7,5},{10,8},{11,9},{14,12},{15,13},{18,16},{19,... | collective-permute-start | bytes 786440 | tf_op jit(solution)/shard_map/ppermute | solution.py:28
  67.3 17.0 %collective-permute-start.11 = (bf16[128,8,128]{0,2,1:T(8,128)(2,1)S(1)}, bf16[128,8,128]{0,2,1:T(8,128)(2,1)S(1)}, u32[]{:S(2)}, u32[]{:S(2)}) collective-permute-start(bf16[128,8,128]{0,2,1:T(8,128)(2,1)S(1)} %get-tuple-element.46), channel_id=1, source_target_pairs={{3,0},{7,4},{11,8},{15,12},{19,16},{23,20},{27,24},{31,28}} | collective-permute-start | bytes 786440 | tf_op jit(solution)/shard_map/ppermute | solution.py:28
  68.6 15.6 %collective-permute-start.9 = (bf16[128,8,128]{0,2,1:T(8,128)(2,1)S(1)}, bf16[128,8,128]{0,2,1:T(8,128)(2,1)S(1)}, u32[]{:S(2)}, u32[]{:S(2)}) collective-permute-start(bf16[128,8,128]{0,2,1:T(8,128)(2,1)S(1)} %get-tuple-element.45), channel_id=1, source_target_pairs={{1,0},{2,1},{3,2},{5,4},{6,5},{7,6},{9,8},{10,9},{11,10},{13,12},{... | collective-permute-start | bytes 786440 | tf_op jit(solution)/shard_map/ppermute | solution.py:28
  85.6 27.7 %copy-start.4 = (bf16[1,128,1024]{2,1,0:T(8,128)(2,1)}, bf16[1,128,1024]{2,1,0:T(8,128)(2,1)S(1)}, u32[]{:S(2)}) copy-start(bf16[1,128,1024]{2,1,0:T(8,128)(2,1)S(1)} %copy.210) | copy-start | bytes 786436
  86.7 26.5 %collective-permute-start.12 = (bf16[1,128,4096]{2,1,0:T(8,128)(2,1)S(1)}, bf16[1,128,4096]{2,1,0:T(8,128)(2,1)S(1)}, u32[]{:S(2)}, u32[]{:S(2)}) collective-permute-start(bf16[1,128,4096]{2,1,0:T(8,128)(2,1)S(1)} %get-tuple-element.38), channel_id=1, source_target_pairs={{0,28},{4,0},{8,4},{12,8},{16,12},{20,16},{24,20},{28,24},{1,29},{... | collective-permute-start | bytes 3145736 | tf_op jit(solution)/shard_map/ppermute | solution.py:18
  113.4 46.1 %collective-permute-start.13 = (bf16[2,128,4096]{2,1,0:T(8,128)(2,1)S(1)}, bf16[2,128,4096]{2,1,0:T(8,128)(2,1)S(1)}, u32[]{:S(2)}, u32[]{:S(2)}) collective-permute-start(bf16[2,128,4096]{2,1,0:T(8,128)(2,1)S(1)} %pad_maximum_fusion.1), channel_id=1, source_target_pairs={{0,24},{4,28},{8,0},{12,4},{16,8},{20,12},{24,16},{28,20},{1,25},{... | collective-permute-start | bytes 6291464 | tf_op jit(solution)/shard_map/ppermute | solution.py:18
  162.6 220.2 %collective-permute-start.14 = (bf16[4,128,4096]{2,1,0:T(8,128)(2,1)}, bf16[4,128,4096]{2,1,0:T(8,128)(2,1)}, u32[]{:S(2)}, u32[]{:S(2)}) collective-permute-start(bf16[4,128,4096]{2,1,0:T(8,128)(2,1)} %pad_maximum_fusion), channel_id=1, source_target_pairs={{0,16},{4,20},{8,24},{12,28},{16,0},{20,4},{24,8},{28,12},{1,17},{... | collective-permute-start | bytes 12582920 | tf_op jit(solution)/shard_map/ppermute | solution.py:18
  205.9 167.4 %all-to-all-start.1 = ((bf16[8,2,43008]{2,1,0:T(2,128)(2,1)}), bf16[8,2,43008]{2,1,0:T(2,128)(2,1)}, u32[]{:S(2)}, u32[]{:S(2)}) async-start(bf16[8,2,43008]{2,1,0:T(2,128)(2,1)} %reshape.256), calls=%async_computation.1 | async-start | bytes 2752512 | tf_op jit(solution)/shard_map/all_to_all | solution.py:62
  214.2 265.5 %reduce-scatter.2.cloned.1.call-start = ((), (), s32[]{:S(2)}) async-start(), calls=%async_computation.3 | async-start | bytes 6881280 | tf_op jit(solution)/shard_map/reduce_scatter | solution.py:137
  382.8 4.7 copy-start.1
  382.8 4.7 copy-start.5
  416.7 61.5 %all-to-all-start = ((bf16[8,128,672]{1,2,0:T(8,128)(2,1)}), bf16[8,128,672]{1,2,0:T(8,128)(2,1)S(1)}, u32[]{:S(2)}, u32[]{:S(2)}) async-start(bf16[8,128,672]{1,2,0:T(8,128)(2,1)} %fusion.23), calls=%async_computation | async-start | bytes 2752512 | tf_op jit(solution)/shard_map/all_to_all | solution.py:134
Sparse Core Ops, SparseCore 0:
  406.0 57.5 reduce-scatter.1
